TPU v7x, 32 devices: a whole 2x2x4 slice. The times are simulated.
32 devices in a mesh: tm: 4 (over y, core), scen: 8 (over z, x).
Axes of the slice: x: 2, y: 2, z: 4, core: 2. Of those that a mesh axis runs over, the one named last changes fastest.
Arguments:
- prior_dispatch: float32 [600, 8192], P(None, ('tm', 'scen')), may hold values from 0 to 1
- prior_commitment: float32 [600, 8192], P(None, ('tm', 'scen')), may hold values from 0 to 1
- prior_consensus: float32 [600, 32], P(None, 'tm'), may hold values from 0 to 1
- prior_multiplier: float32 [600, 8192], P(None, ('tm', 'scen')), may hold values from -2 to 2
- flow_factors: bfloat16 [2560, 2000], P('scen'), may hold values from -0.25 to 0.25
- unit_buses: int32 [600], replicated, may hold values from 0 to 1999
- wind_buses: int32 [128], replicated, may hold values from 0 to 1999
- wind_output: bfloat16 [128, 8192], P(None, ('tm', 'scen')), may hold values from 0 to 1
- demand: float32 [32], P('tm'), may hold values from 180 to 300
- load_flows: bfloat16 [2560, 32], P('scen', 'tm'), may hold values from -6 to 6
- line_limits: bfloat16 [2560], P('scen'), may hold values from 0.29882812 to 3
- unit_table: float32 [5, 600], replicated, may hold values from 0.05 to 2, as said below
Outputs:
- dispatch: float32 [600, 8192], P(None, ('tm', 'scen'))
- commitment: float32 [600, 8192], P(None, ('tm', 'scen'))
- consensus: float32 [600, 32], P(None, 'tm')
- multiplier: float32 [600, 8192], P(None, ('tm', 'scen'))
Inputs may be any that keep to these rules, and one draw needn't show every extreme that they name: `unit_table`: rows 0 and 4 lie in 0.1 to 1, row 1 in 0.05 to 0.5, row 2 in 0.5 to 2, row 3 in 0.05 to 0.5.
All inputs are finite; a program needn't handle non-finite values.
Results may differ from a plain program's by a relative error of at most 0.0017.
Values may be sent and summed in bfloat16 or wider, within the bound.
A program may use at most 64 MiB of HBM per device.

v0:
```python
import jax
import jax.numpy as jnp
from jax import lax
from jax.sharding import PartitionSpec as P

UNITS = 600
PASSES = 3
H_DEV = 8


flow_weight = 0.5
ramp_weight = 1.0
balance_weight = 0.004
short_weight = 2.0
penalty = 1.0
step_power = 0.2
step_commit = 0.3


def passed_along(value, axis, steps):
    count = lax.axis_size(axis)
    first, last = (max(0, -steps), min(count, count - steps))
    return lax.ppermute(value, axis, [(source, source + steps) for source in range(first, last)])


def make_fold(extended, block):

    def fold_lines(total, pieces, start):
        piece, hourly, bound = pieces
        flows = jnp.dot(piece, extended, preferred_element_type=jnp.float32)
        flows = flows - jnp.repeat(hourly.astype(jnp.float32), block, axis=1)
        limit_col = bound.astype(jnp.float32)[:, None]
        excess = flows - jnp.clip(flows, -limit_col, limit_col)
        return lax.dot_general(
            piece[:, :UNITS],
            excess.astype(jnp.bfloat16),
            (((0,), (0,)), ((), ())),
            preferred_element_type=jnp.float32,
        )

    return fold_lines


def per_device(
    prior_dispatch,
    prior_commitment,
    prior_consensus,
    prior_multiplier,
    flow_factors,
    unit_buses,
    wind_buses,
    wind_output,
    demand,
    load_flows,
    line_limits,
    unit_table,
):
    columns = prior_dispatch.shape[1]
    block = columns // H_DEV
    linear = unit_table[0][:, None]
    quadratic = unit_table[1][:, None]
    capacity = unit_table[2][:, None]
    ramp_limit = unit_table[3][:, None]
    noload = unit_table[4][:, None]
    factors = jnp.concatenate(
        [jnp.take(flow_factors, unit_buses, axis=1), jnp.take(flow_factors, wind_buses, axis=1)],
        axis=1,
    )
    wind_total = jnp.sum(wind_output.astype(jnp.float32), axis=0)
    needed = jnp.repeat(demand, block)
    target = jnp.repeat(prior_consensus, block, axis=1)
    first_block = lax.axis_index("tm") == 0
    last_block = lax.axis_index("tm") == lax.axis_size("tm") - 1
    empty = jnp.zeros((UNITS, columns), jnp.float32)
    power = prior_dispatch
    commit = prior_commitment
    extended = jnp.concatenate([power.astype(jnp.bfloat16), wind_output], axis=0)
    fold_lines = make_fold(extended, block)
    all_rows = (
        lax.all_gather(factors, "scen", axis=0, tiled=True),
        lax.all_gather(load_flows, "scen", axis=0, tiled=True),
        lax.all_gather(line_limits, "scen", axis=0, tiled=True),
    )
    back = fold_lines(empty, all_rows, 0)
    for number in range(PASSES):
        if number > 0:
            extended = jnp.concatenate([power.astype(jnp.bfloat16), wind_output], axis=0)
            back = make_fold(extended, block)(empty, all_rows, 0)
        before = passed_along(power[:, columns - block :], "tm", 1)
        after = passed_along(power[:, :block], "tm", -1)
        before = jnp.where(first_block, power[:, :block], before)
        previous = jnp.concatenate([before, power[:, : columns - block]], axis=1)
        rate = power - previous
        over = rate - jnp.clip(rate, -ramp_limit, ramp_limit)
        edge = after - power[:, columns - block :]
        edge_over = edge - jnp.clip(edge, -ramp_limit, ramp_limit)
        edge_over = jnp.where(last_block, jnp.zeros_like(edge_over), edge_over)
        following = jnp.concatenate([over[:, block:], edge_over], axis=1)
        ramp_term = over - following
        balance = jnp.sum(power, axis=0) + wind_total - needed
        short = jnp.maximum(power - capacity * commit, 0.0)
        grad_power = (
            linear
            + 2.0 * quadratic * power
            + flow_weight * back
            + ramp_weight * ramp_term
            + balance_weight * balance
            + short_weight * short
        )
        grad_commit = (
            noload
            - short_weight * capacity * short
            + prior_multiplier
            + penalty * (commit - target)
        )
        new_power = jnp.clip(power - step_power * grad_power, 0.0, capacity)
        new_commit = jnp.clip(commit - step_commit * grad_commit, 0.0, 1.0)
        power = new_power
        commit = new_commit
    partial_sums = jnp.sum(
        (commit + prior_multiplier / penalty).reshape(UNITS, H_DEV, block), axis=2
    )
    scenario_count = block * lax.axis_size("scen")
    totals = lax.psum(partial_sums, "scen")
    consensus = jnp.clip(totals / scenario_count, 0.0, 1.0)
    updated = prior_multiplier + penalty * (commit - jnp.repeat(consensus, block, axis=1))
    return (power, commit, consensus, updated)


def solution(mesh):
    in_specs = (
        P(None, ("tm", "scen")),
        P(None, ("tm", "scen")),
        P(None, "tm"),
        P(None, ("tm", "scen")),
        P("scen", None),
        P(),
        P(),
        P(None, ("tm", "scen")),
        P("tm"),
        P("scen", "tm"),
        P("scen"),
        P(),
    )
    out_specs = (
        P(None, ("tm", "scen")),
        P(None, ("tm", "scen")),
        P(None, "tm"),
        P(None, ("tm", "scen")),
    )
    return jax.shard_map(
        per_device, mesh=mesh, in_specs=in_specs, out_specs=out_specs, check_vma=False
    )
```

profile of v0, /device:TPU:4, one launch (start us, length us, event | category | flops | bytes accessed | tf_op | source)
XLA Modules:
  0.0 190.7 jit_solution(6578363488554750954)
XLA Ops:
  9.9 2.4 %copy.31 = bf16[320,2000]{0,1:T(8,128)(2,1)S(1)} copy(bf16[320,2000]{1,0:T(8,128)(2,1)} %param.16) | data formatting | bytes 2560000 | tf_op args[4]
  13.2 2.8 %gather_fusion = bf16[600,320]{1,0:T(8,128)(2,1)S(1)} fusion(bf16[320,2000]{0,1:T(8,128)(2,1)S(1)} %copy.31, s32[1024]{0:T(1024)S(1)} %pad_clamp_fusion.1), kind=kCustom, calls=%fused_computation | custom fusion | bytes 770400 | tf_op jit(solution)/shard_map/jit(_take)/gather | solution.py:66
  18.4 1.9 %collective-permute-start.1 = (f32[600,32]{1,0:T(8,128)}, f32[600,32]{1,0:T(8,128)}, u32[]{:S(2)}, u32[]{:S(2)}) collective-permute-start(f32[600,32]{1,0:T(8,128)} %get-tuple-element.31), channel_id=1, source_target_pairs={{8,0},{16,8},{24,16},{9,1},{17,9},{25,17},{10,2},{18,10},{26,18},{... | collective-permute-start | bytes 230408 | tf_op jit(solution)/shard_map/ppermute | solution.py:23
  20.3 3.1 %collective-permute-start = (f32[600,32]{1,0:T(8,128)}, f32[600,32]{1,0:T(8,128)}, u32[]{:S(2)}, u32[]{:S(2)}) collective-permute-start(f32[600,32]{1,0:T(8,128)} %get-tuple-element.32), channel_id=1, source_target_pairs={{0,8},{8,16},{16,24},{1,9},{9,17},{17,25},{2,10},{10,18},{18,26},{... | collective-permute-start | bytes 230408 | tf_op jit(solution)/shard_map/ppermute | solution.py:23
  23.4 31.7 %all-gather = bf16[8,320,8]{1,2,0:T(8,128)(2,1)S(1)} all-gather(bf16[1,320,8]{1,2,0:T(8,128)(2,1)S(1)} %bitcast.25), channel_id=1, replica_groups=mesh['tm'=4,'scen'=8] {'scen'}, dimensions={0}, use_global_device_ids=true | all-gather | bytes 46080 | tf_op jit(solution)/shard_map/all_gather | solution.py:81
  55.6 2.1 %copy.35 = f32[2560,256]{1,0:T(8,128)} copy(f32[2560,256]{0,1:T(8,128)S(1)} %bitcast.21) | data formatting | bytes 5242880 | tf_op jit(solution)/shard_map/reshape | solution.py:31
  59.2 22.3 %all-reduce = bf16[2560]{0:T(1024)(128)(2,1)S(1)} all-reduce(bf16[2560]{0:T(1024)(128)(2,1)S(1)} %dynamic-update-slice), channel_id=1, replica_groups=mesh['tm'=4,'scen'=8] {'scen'}, use_global_device_ids=true, to_apply=%add | all-reduce | flops 2560 | bytes 10240
  81.9 1.4 subtract_select_fusion.2
  84.6 5.3 %all-gather.3.cloned.1.call-done = bf16[2560,728]{1,0:T(8,128)(2,1)} async-done(((bf16[320,728]{1,0:T(8,128)(2,1)}), bf16[2560,728]{1,0:T(8,128)(2,1)}) %all-gather.3.cloned.1.call-update) | async-done | bytes 3727376 | tf_op jit(solution)/shard_map/all_gather | solution.py:80
  89.9 7.5 %fusion.84 = f32[600,256]{1,0:T(8,128)S(1)} fusion(f32[600,256]{1,0:T(8,128)S(1)} %copy-done, bf16[2560,728]{1,0:T(8,128)(2,1)} %all-gather.3.cloned.1.call-done, f32[2560,256]{1,0:T(8,128)} %copy.35, f32[2560]{0:T(1024)S(1)} %convert_negate_fusion, f32[2560]{0:T(1024)S(1)} %convert_element_type.33, f32[600,256]{1,0:T(8,128)S(1)} %get-tuple-element.27, ...), kind=kOutput, calls=%fused_computation.40 | convolution fusion | flops 1747269632 | bytes 13303840 | tf_op jit(solution)/shard_map/dot_general | solution.py:34
  98.3 1.9 %collective-permute-start.3 = (f32[600,32]{1,0:T(8,128)}, f32[600,32]{1,0:T(8,128)S(1)}, u32[]{:S(2)}, u32[]{:S(2)}) collective-permute-start(f32[600,32]{1,0:T(8,128)} %get-tuple-element.24), channel_id=1, source_target_pairs={{8,0},{16,8},{24,16},{9,1},{17,9},{25,17},{10,2},{18,10},{26,18},{... | collective-permute-start | bytes 230408 | tf_op jit(solution)/shard_map/ppermute | solution.py:23
  100.2 2.6 %collective-permute-start.2 = (f32[600,32]{1,0:T(8,128)}, f32[600,32]{1,0:T(8,128)}, u32[]{:S(2)}, u32[]{:S(2)}) collective-permute-start(f32[600,32]{1,0:T(8,128)} %get-tuple-element.25), channel_id=1, source_target_pairs={{0,8},{8,16},{16,24},{1,9},{9,17},{17,25},{2,10},{10,18},{18,26},{... | collective-permute-start | bytes 230408 | tf_op jit(solution)/shard_map/ppermute | solution.py:23
  103.2 1.7 collective-permute-done.3
  104.9 3.8 %collective-permute-done.2 = f32[600,32]{1,0:T(8,128)} collective-permute-done((f32[600,32]{1,0:T(8,128)}, f32[600,32]{1,0:T(8,128)}, u32[]{:S(2)}, u32[]{:S(2)}) %collective-permute-start.2) | collective-permute-done | bytes 76832 | tf_op jit(solution)/shard_map/ppermute | solution.py:23
  108.7 2.0 %subtract_select_fusion.1 = (f32[600,32]{1,0:T(8,128)}, f32[600,32]{1,0:T(8,128)S(1)}) fusion(f32[600,32]{1,0:T(8,128)S(1)} %collective-permute-done.3, f32[600]{0:T(1024)S(1)} %neg.20, f32[600]{0:T(1024)S(1)} %get-tuple-element.8, pred[]{:T(512)S(6)} %eq.7, f32[600,256]{1,0:T(8,128)S(1)} %fusion.84, f32[600,32]{1,0:T(8,128)} %collective-permute-done.2, ...), kind=kLoop, calls=%fused_computation.67 | loop fusion | flops 115200 | bytes 465602 | tf_op jit(solution)/shard_map/jit(_where)/select_n | solution.py:97
  112.9 8.0 %fusion.69 = f32[600,256]{1,0:T(8,128)S(1)} fusion(f32[600,256]{1,0:T(8,128)S(1)} %fusion.84, bf16[2560,728]{1,0:T(8,128)(2,1)} %all-gather.3.cloned.1.call-done, f32[2560,256]{1,0:T(8,128)} %copy.35, f32[2560]{0:T(1024)S(1)} %copy-done.13, f32[2560]{0:T(1024)S(1)} %convert_element_type.33, f32[600,256]{1,0:T(8,128)} %copy-done.5, ...), kind=kOutput, calls=%fused_computation.35 | convolution fusion | flops 1748959232 | bytes 15228640 | tf_op jit(solution)/shard_map/dot_general | solution.py:34
  121.1 2.0 %collective-permute-start.5 = (f32[600,32]{1,0:T(8,128)S(1)}, f32[600,32]{1,0:T(8,128)S(1)}, u32[]{:S(2)}, u32[]{:S(2)}) collective-permute-start(f32[600,32]{1,0:T(8,128)S(1)} %get-tuple-element.17), channel_id=1, source_target_pairs={{8,0},{16,8},{24,16},{9,1},{17,9},{25,17},{10,2},{18,10},{26,18},{... | collective-permute-start | bytes 230408 | tf_op jit(solution)/shard_map/ppermute | solution.py:23
  123.2 2.4 %collective-permute-start.4 = (f32[600,32]{1,0:T(8,128)S(1)}, f32[600,32]{1,0:T(8,128)S(1)}, u32[]{:S(2)}, u32[]{:S(2)}) collective-permute-start(f32[600,32]{1,0:T(8,128)S(1)} %get-tuple-element.18), channel_id=1, source_target_pairs={{0,8},{8,16},{16,24},{1,9},{9,17},{17,25},{2,10},{10,18},{18,26},{... | collective-permute-start | bytes 230408 | tf_op jit(solution)/shard_map/ppermute | solution.py:23
  125.6 1.9 %collective-permute-done.5 = f32[600,32]{1,0:T(8,128)S(1)} collective-permute-done((f32[600,32]{1,0:T(8,128)S(1)}, f32[600,32]{1,0:T(8,128)S(1)}, u32[]{:S(2)}, u32[]{:S(2)}) %collective-permute-start.5) | collective-permute-done | bytes 76832 | tf_op jit(solution)/shard_map/ppermute | solution.py:23
  127.5 3.8 %collective-permute-done.4 = f32[600,32]{1,0:T(8,128)S(1)} collective-permute-done((f32[600,32]{1,0:T(8,128)S(1)}, f32[600,32]{1,0:T(8,128)S(1)}, u32[]{:S(2)}, u32[]{:S(2)}) %collective-permute-start.4) | collective-permute-done | bytes 76832 | tf_op jit(solution)/shard_map/ppermute | solution.py:23
  132.4 2.2 %fusion.99 = (f32[600,256]{1,0:T(8,128)}, f32[600,256]{1,0:T(8,128)}, f32[600,256]{1,0:T(8,128)}, f32[256]{0:T(256)S(1)}, bf16[600,256]{1,0:T(8,128)(2,1)S(1)}, /*index=5*/f32[600,256]{1,0:T(8,128)S(1)}) fusion(f32[600,256]{1,0:T(8,128)S(1)} %copy-done.1, f32[600,256]{1,0:T(8,128)S(1)} %copy.37, f32[600,256]{1,0:T(8,128)S(1)} %fusion.69, ...), kind=kLoop, calls=%fused_computation.94 | loop fusion | flops 6297344 | bytes 7078624 | tf_op jit(solution)/shard_map/add | solution.py:121
  137.0 35.0 %psum.7 = f32[600,8]{0,1:T(8,128)S(1)} all-reduce(f32[600,8]{0,1:T(8,128)S(1)} %bitcast_reduce_fusion), channel_id=1, replica_groups=mesh['tm'=4,'scen'=8] {'scen'}, use_global_device_ids=true, to_apply=%region_5.6 | all-reduce | flops 4800 | bytes 38400 | tf_op jit(solution)/shard_map/psum | solution.py:124
  173.2 2.1 %subtract_add_fusion = f32[600,256]{1,0:T(8,128)} fusion(f32[600,256]{1,0:T(8,128)S(1)} %copy-done.1, f32[600,256]{1,0:T(8,128)S(1)} %copy-done.2, f32[600,256]{1,0:T(8,128)} %copy.42), kind=kLoop, calls=%fused_computation.48 | loop fusion | flops 307200 | bytes 2457600 | tf_op jit(solution)/shard_map/add | solution.py:126
  175.3 8.6 %fusion.54 = f32[600,256]{1,0:T(8,128)} fusion(f32[600,256]{1,0:T(8,128)S(1)} %fusion.69, bf16[2560,728]{1,0:T(8,128)(2,1)} %all-gather.3.cloned.1.call-done, f32[2560,256]{1,0:T(8,128)} %copy.35, f32[2560]{0:T(1024)S(1)} %copy-done.13, f32[2560]{0:T(1024)S(1)} %convert_element_type.33, f32[600,256]{1,0:T(8,128)S(1)} %copy-done.4, ...), kind=kOutput, calls=%fused_computation.30 | convolution fusion | flops 1747269632 | bytes 13611040 | tf_op jit(solution)/shard_map/dot_general | solution.py:34
  (86 shorter events, 16.8 us)
Async XLA Ops:
  7.2 82.7 %all-gather.3.cloned.1.call-start = ((), (), s32[]{:S(2)}) async-start(), calls=%async_computation | async-start | bytes 4423680 | tf_op jit(solution)/shard_map/all_gather | solution.py:80
  16.0 1.4 copy-start
  16.1 7.4 %copy-start.15 = (bf16[320,8]{0,1:T(8,128)(2,1)S(1)}, bf16[320,8]{0,1:T(8,128)(2,1)}, u32[]{:S(2)}) copy-start(bf16[320,8]{0,1:T(8,128)(2,1)} %param.21) | copy-start | bytes 15364
  18.4 63.5 %collective-permute-start.1 = (f32[600,32]{1,0:T(8,128)}, f32[600,32]{1,0:T(8,128)}, u32[]{:S(2)}, u32[]{:S(2)}) collective-permute-start(f32[600,32]{1,0:T(8,128)} %get-tuple-element.31), channel_id=1, source_target_pairs={{8,0},{16,8},{24,16},{9,1},{17,9},{25,17},{10,2},{18,10},{26,18},{... | collective-permute-start | bytes 230408 | tf_op jit(solution)/shard_map/ppermute | solution.py:23
  20.3 61.6 %collective-permute-start = (f32[600,32]{1,0:T(8,128)}, f32[600,32]{1,0:T(8,128)}, u32[]{:S(2)}, u32[]{:S(2)}) collective-permute-start(f32[600,32]{1,0:T(8,128)} %get-tuple-element.32), channel_id=1, source_target_pairs={{0,8},{8,16},{16,24},{1,9},{9,17},{17,25},{2,10},{10,18},{18,26},{... | collective-permute-start | bytes 230408 | tf_op jit(solution)/shard_map/ppermute | solution.py:23
  55.5 2.2 %copy-start.18 = (u32[32]{0:T(128)S(1)}, u32[32]{0:T(128)}, u32[]{:S(2)}) copy-start(u32[32]{0:T(128)} %constant.59) | copy-start | bytes 388
  55.5 3.4 %copy-start.16 = (bf16[320]{0:T(512)(128)(2,1)S(1)}, bf16[320]{0:T(512)(128)(2,1)}, u32[]{:S(2)}) copy-start(bf16[320]{0:T(512)(128)(2,1)} %param.22) | copy-start | bytes 1924
  55.5 26.0 %copy-start.14 = (f32[5,600]{1,0:T(8,128)S(1)}, f32[5,600]{1,0:T(8,128)}, u32[]{:S(2)}) copy-start(f32[5,600]{1,0:T(8,128)} %param.23) | copy-start | bytes 36004
  55.6 26.1 %copy-start.17 = (f32[8]{0:T(128)S(1)}, f32[8]{0:T(128)}, u32[]{:S(2)}) copy-start(f32[8]{0:T(128)} %param.20) | copy-start | bytes 100
  55.6 26.2 %copy-start.10 = (bf16[128,256]{1,0:T(8,128)(2,1)S(1)}, bf16[128,256]{1,0:T(8,128)(2,1)}, u32[]{:S(2)}) copy-start(bf16[128,256]{1,0:T(8,128)(2,1)} %param.19) | copy-start | bytes 196612
  81.8 8.1 %copy-start.12 = (f32[2560]{0:T(1024)}, f32[2560]{0:T(1024)S(1)}, u32[]{:S(2)}) copy-start(f32[2560]{0:T(1024)S(1)} %convert_negate_fusion) | copy-start | bytes 30724
  81.8 8.1 %copy-start.6 = (f32[600,256]{1,0:T(8,128)S(1)}, f32[600,256]{1,0:T(8,128)}, u32[]{:S(2)}) copy-start(f32[600,256]{1,0:T(8,128)} %param.13) | copy-start | bytes 1843204
  89.9 13.0 %copy-start.11 = (f32[600,8]{0,1:T(8,128)S(1)}, f32[600,8]{0,1:T(8,128)}, u32[]{:S(2)}) copy-start(f32[600,8]{0,1:T(8,128)} %param.14) | copy-start | bytes 57604
  98.3 6.6 %collective-permute-start.3 = (f32[600,32]{1,0:T(8,128)}, f32[600,32]{1,0:T(8,128)S(1)}, u32[]{:S(2)}, u32[]{:S(2)}) collective-permute-start(f32[600,32]{1,0:T(8,128)} %get-tuple-element.24), channel_id=1, source_target_pairs={{8,0},{16,8},{24,16},{9,1},{17,9},{25,17},{10,2},{18,10},{26,18},{... | collective-permute-start | bytes 230408 | tf_op jit(solution)/shard_map/ppermute | solution.py:23
  100.2 8.5 %collective-permute-start.2 = (f32[600,32]{1,0:T(8,128)}, f32[600,32]{1,0:T(8,128)}, u32[]{:S(2)}, u32[]{:S(2)}) collective-permute-start(f32[600,32]{1,0:T(8,128)} %get-tuple-element.25), channel_id=1, source_target_pairs={{0,8},{8,16},{16,24},{1,9},{9,17},{17,25},{2,10},{10,18},{18,26},{... | collective-permute-start | bytes 230408 | tf_op jit(solution)/shard_map/ppermute | solution.py:23
  103.2 9.8 %copy-start.1 = (f32[600,256]{1,0:T(8,128)S(1)}, f32[600,256]{1,0:T(8,128)}, u32[]{:S(2)}) copy-start(f32[600,256]{1,0:T(8,128)} %param.15) | copy-start | bytes 1843204
  103.2 9.7 %copy-start.13 = (f32[2560]{0:T(1024)S(1)}, f32[2560]{0:T(1024)}, u32[]{:S(2)}) copy-start(f32[2560]{0:T(1024)} %copy-done.12) | copy-start | bytes 30724
  110.7 2.2 %copy-start.8 = (f32[600,32]{1,0:T(8,128)S(1)}, f32[600,32]{1,0:T(8,128)}, u32[]{:S(2)}) copy-start(f32[600,32]{1,0:T(8,128)} %get-tuple-element.22) | copy-start | bytes 230404
  121.0 11.4 %copy-start.7 = (f32[600,256]{1,0:T(8,128)S(1)}, f32[600,256]{1,0:T(8,128)}, u32[]{:S(2)}) copy-start(f32[600,256]{1,0:T(8,128)} %param.13) | copy-start | bytes 1843204
  121.1 6.4 %collective-permute-start.5 = (f32[600,32]{1,0:T(8,128)S(1)}, f32[600,32]{1,0:T(8,128)S(1)}, u32[]{:S(2)}, u32[]{:S(2)}) collective-permute-start(f32[600,32]{1,0:T(8,128)S(1)} %get-tuple-element.17), channel_id=1, source_target_pairs={{8,0},{16,8},{24,16},{9,1},{17,9},{25,17},{10,2},{18,10},{26,18},{... | collective-permute-start | bytes 230408 | tf_op jit(solution)/shard_map/ppermute | solution.py:23
  123.2 8.2 %collective-permute-start.4 = (f32[600,32]{1,0:T(8,128)S(1)}, f32[600,32]{1,0:T(8,128)S(1)}, u32[]{:S(2)}, u32[]{:S(2)}) collective-permute-start(f32[600,32]{1,0:T(8,128)S(1)} %get-tuple-element.18), channel_id=1, source_target_pairs={{0,8},{8,16},{16,24},{1,9},{9,17},{17,25},{2,10},{10,18},{18,26},{... | collective-permute-start | bytes 230408 | tf_op jit(solution)/shard_map/ppermute | solution.py:23
  134.6 38.6 %copy-start.2 = (f32[600,256]{1,0:T(8,128)S(1)}, f32[600,256]{1,0:T(8,128)}, u32[]{:S(2)}) copy-start(f32[600,256]{1,0:T(8,128)} %get-tuple-element.10) | copy-start | bytes 1843204
  137.0 38.3 %copy-start.4 = (f32[600,256]{1,0:T(8,128)S(1)}, f32[600,256]{1,0:T(8,128)}, u32[]{:S(2)}) copy-start(f32[600,256]{1,0:T(8,128)} %copy-done.3) | copy-start | bytes 1843204
  172.1 11.8 %copy-start.9 = (f32[600,8]{0,1:T(8,128)}, f32[600,8]{0,1:T(8,128)S(1)}, u32[]{:S(2)}) copy-start(f32[600,8]{0,1:T(8,128)S(1)} %multiply_clamp_fusion) | copy-start | bytes 57604
  (2 other events, 2.1 us)
Sparse Core Ops, SparseCore 0:
  17.6 72.2 all-gather.2
where the time goes:
time: 191 us
  blocking collectives  89 us (47%)
  matrix products  24.1 us (13%)
  local copies, waits for them, and re-layouts  17.7 us (9%)
  waiting for transfers between devices  16.6 us (9%)
  between operations  15.1 us (8%)
  starting transfers between devices  14.1 us (7%)
  other arithmetic  14.1 us (7%)
    psum x1, blocking collectives, per_device(): totals = lax.psum(partial_sums, 'scen')  35 us
    all_gather x1, blocking collectives, per_device(): lax.all_gather(load_flows, 'scen', axis=0, tiled=True)  31.7 us
    dot_general x3, matrix products, fold_lines(): lax.dot_general(piece[:, :UNITS], excess.astype(jnp.bfloat16), (((0,), (0...  24.1 us
    unnamed x1, blocking collectives  22.3 us
    ppermute x6, starting transfers between devices, passed_along(): lax.ppermute(value, axis, [(source, source + steps) for source in range(f...  14 us
    ppermute x6, waiting for transfers between devices, passed_along(): lax.ppermute(value, axis, [(source, source + steps) for source in range(f...  11.3 us
    all_gather x1, waiting for transfers between devices, per_device(): lax.all_gather(factors, 'scen', axis=0, tiled=True)  5.26 us
    select_n x3, other arithmetic, per_device(): edge_over = jnp.where(last_block, jnp.zeros_like(edge_over), edge_over)  4.48 us
  transfers between devices with their start and end apart: 7, of which 5 were waited for; matrix products, arithmetic and copies ran while one was open for 4% of the time, Pallas kernels for 0%

commit v1 on v0

v1 whole, which is shorter than its diff:
```python
import functools

import jax
import jax.numpy as jnp
from jax import lax
from jax.experimental import pallas as pl
from jax.experimental.pallas import tpu as pltpu
from jax.sharding import PartitionSpec as P

PASSES = 3
H_DEV = 8
MESH = pl.DeviceIdType.MESH

flow_weight = 0.5
ramp_weight = 1.0
balance_weight = 0.004
short_weight = 2.0
penalty = 1.0
step_power = 0.2
step_commit = 0.3


def kernel(n_tm, n_scen, units, sel_ref, tab_ref, pd_ref, pc_ref, cons_ref, mu_ref, wind_ref, need_ref, ut_ref,
           power_out, commit_out, cons_out, upd_out,
           fac, fact, load, bound, exc, pw, cm, mult, target, ext, backs, bef, aft,
           tabs, esend, erecv, psend, precv, total_row,
           recv_sem, send_sem, tsend, trecv, esem_s, esem_r, psem_s, psem_r):
    rows = sel_ref.shape[0]
    quarter = rows // 4
    up = pw.shape[0]
    cols = pw.shape[1]
    block = cols // H_DEV
    chunk = 2 * rows
    n_z = n_scen // 2
    f32, bf16 = jnp.float32, jnp.bfloat16
    tm = lax.axis_index("tm")
    scen = lax.axis_index("scen")
    y, c = tm // 2, tm % 2
    z, x = scen // 2, scen % 2
    oy = 1 - y
    oc = 1 - c
    ox = 1 - x
    mine = y * 2 + c
    other = oy * 2 + c
    dev_x = (tm, z * 2 + ox)
    dev_y = (oy * 2 + c, scen)
    dev_c = (y * 2 + oc, scen)
    dev_dn = (tm, scen - 2)
    dev_up = (tm, scen + 2)

    def piece(zz, xx, q):
        return (zz * 2 + xx) * 4 + q

    def at(p):
        return fac.at[pl.ds(pl.multiple_of(p * quarter, 16), quarter), :]

    def own(q):
        return sel_ref.at[pl.ds(pl.multiple_of(q * quarter, 16), quarter), :]

    def copy(src, p, slot, dev):
        return pltpu.make_async_remote_copy(
            src_ref=src, dst_ref=at(p), send_sem=send_sem.at[slot, p], recv_sem=recv_sem.at[p],
            device_id=dev, device_id_type=MESH)

    def pass_on(p, slot, dev):
        copy(at(p), p, slot, dev).start()

    def arrived(p):
        copy(at(p), p, 0, dev_x).wait_recv()

    def table_copy(k):
        peer = lax.rem(scen + k, n_scen)
        return pltpu.make_async_remote_copy(
            src_ref=tab_ref, dst_ref=tabs.at[scen], send_sem=tsend.at[k], recv_sem=trecv.at[scen],
            device_id=(tm, peer), device_id_type=MESH)

    barrier = pltpu.get_barrier_semaphore()
    for k in range(1, n_scen):
        pl.semaphore_signal(barrier, inc=1, device_id=(tm, lax.rem(scen + k, n_scen)), device_id_type=MESH)
    for k in range(1, n_tm):
        pl.semaphore_signal(barrier, inc=1, device_id=(lax.rem(tm + k, n_tm), scen), device_id_type=MESH)
    pl.semaphore_wait(barrier, n_scen - 1 + n_tm - 1)

    p_own = piece(z, x, mine)
    p_own2 = piece(z, x, other)

    @pl.when(z > 0)
    def _():
        copy(own(mine), p_own, 0, dev_dn).start()

    @pl.when(z < n_z - 1)
    def _():
        copy(own(mine), p_own, 1, dev_up).start()

    copy(own(mine), p_own, 2, dev_x).start()
    copy(own(other), p_own2, 2, dev_x).start()
    for k in range(1, n_scen):
        table_copy(k).start()

    def edges_of(tile_last, tile_first):
        lane = lax.broadcasted_iota(jnp.int32, (up // 4, 128), 1)
        last = jnp.zeros((up // 4, 128), f32)
        first = jnp.zeros((up // 4, 128), f32)
        for g in range(4):
            inside = (lane >= 32 * g) & (lane < 32 * g + 32)
            a = tile_last[g * (up // 4):(g + 1) * (up // 4), :]
            b = tile_first[g * (up // 4):(g + 1) * (up // 4), :]
            sa = (32 * g - 96) % 128
            sb = (32 * g) % 128
            a = pltpu.roll(a, sa, 1) if sa else a
            b = pltpu.roll(b, sb, 1) if sb else b
            last = jnp.where(inside, a, last)
            first = jnp.where(inside, b, first)
        return last, first

    def edge_copy(number, way):
        dev = (tm + 1, scen) if way == 0 else (tm - 1, scen)
        return pltpu.make_async_remote_copy(
            src_ref=esend.at[number, way], dst_ref=erecv.at[number, way],
            send_sem=esem_s.at[number, way], recv_sem=esem_r.at[number, way],
            device_id=dev, device_id_type=MESH)

    def send_edges(number):
        @pl.when(tm < n_tm - 1)
        def _():
            edge_copy(number, 0).start()

        @pl.when(tm > 0)
        def _():
            edge_copy(number, 1).start()

    def store_edges(number):
        last, first = edges_of(pw[:, cols - 128:], pw[:, :128])
        esend[number, 0] = last
        esend[number, 1] = first

    zero_tail = jnp.zeros((up - units, cols), f32)
    pw[:units, :] = pd_ref[...]
    pw[units:, :] = zero_tail
    store_edges(0)
    cm[:units, :] = pc_ref[...]
    cm[units:, :] = zero_tail
    mult[:units, :] = mu_ref[...]
    mult[units:, :] = zero_tail
    hour_row = lax.broadcasted_iota(jnp.int32, (H_DEV, cols), 0)
    hour_col = lax.broadcasted_iota(jnp.int32, (H_DEV, cols), 1)
    hour_of = ((hour_col >= hour_row * block) & (hour_col < hour_row * block + block)).astype(f32)
    target[...] = jnp.dot(cons_ref[...], hour_of, preferred_element_type=f32, precision=lax.Precision.HIGHEST)
    fac[pl.ds(pl.multiple_of(scen * rows, 16), rows), :] = sel_ref[...]
    tabs[scen] = tab_ref[...]
    ext[:up, :] = pw[...].astype(bf16)
    ext[up:, :] = wind_ref[...]
    total_row[...] = jnp.sum(wind_ref[...].astype(f32), axis=0, keepdims=True) - need_ref[...]
    send_edges(0)

    def along_z(k):
        for down in (True, False):
            zz = z - k if down else z + k
            ok = zz >= 0 if down else zz < n_z

            @pl.when(ok)
            def _():
                p = piece(zz, x, mine)
                arrived(p)
                if down:
                    @pl.when(z < n_z - 1)
                    def _():
                        pass_on(p, 1, dev_up)
                else:
                    @pl.when(z > 0)
                    def _():
                        pass_on(p, 0, dev_dn)
                pass_on(p, 2, dev_x)
                pass_on(p, 3, dev_y)
                pass_on(p, 4, dev_c)

    def both(k, f):
        @pl.when(z - k >= 0)
        def _():
            f(z - k)

        @pl.when(z + k < n_z)
        def _():
            f(z + k)

    def across_x(zz):
        p = piece(zz, ox, mine)
        arrived(p)
        pass_on(p, 3, dev_y)
        pass_on(p, 4, dev_c)

    def from_y_same(zz):
        p = piece(zz, x, other)
        arrived(p)
        pass_on(p, 4, dev_c)

    def from_y_cross(zz):
        p = piece(zz, ox, other)
        arrived(p)
        pass_on(p, 4, dev_c)

    def own_plane_x():
        for q in (mine, other):
            p = piece(z, ox, q)
            arrived(p)
            pass_on(p, 4, dev_c)

    along_z(1)
    own_plane_x()
    for k in range(2, n_z + 1):
        if k < n_z:
            along_z(k)
        both(k - 1, across_x)
        both(k - 1, from_y_same)
        if k > 2:
            both(k - 2, from_y_cross)
    both(n_z - 1, from_y_cross)

    def from_core(zz):
        for xx in range(2):
            for yy in range(2):
                arrived(piece(zz, xx, yy * 2 + oc))

    for q in (oc, 2 + oc):
        arrived(piece(z, ox, q))
    for k in range(1, n_z):
        both(k, from_core)
    for k in range(1, n_scen):
        src = lax.rem(scen + k, n_scen)
        pltpu.make_async_remote_copy(
            src_ref=tab_ref, dst_ref=tabs.at[src], send_sem=tsend.at[k], recv_sem=trecv.at[src],
            device_id=dev_x, device_id_type=MESH).wait_recv()

    spread_row = lax.broadcasted_iota(jnp.int32, (16, cols), 0)
    spread_col = lax.broadcasted_iota(jnp.int32, (16, cols), 1)
    load_of = ((spread_col >= spread_row * block) & (spread_col < spread_row * block + block)).astype(bf16)
    limit_of = (spread_row == H_DEV).astype(bf16)
    lines_first = (((0,), (0,)), ((), ()))

    def prepare(s, carry):
        table = tabs[s]
        at_rows = pl.ds(pl.multiple_of(s * rows, 16), rows)
        load[at_rows, :] = lax.dot_general(table, load_of, lines_first, preferred_element_type=f32)[:rows]
        bound[at_rows, :] = lax.dot_general(table, limit_of, lines_first, preferred_element_type=f32)[:rows]
        return carry

    lax.fori_loop(0, n_scen, prepare, 0)

    def flip(k, carry):
        at_rows = pl.ds(pl.multiple_of(k * chunk, 128), chunk)
        fact[:, at_rows] = fac[at_rows, :up].T
        return carry

    lax.fori_loop(0, n_z, flip, 0)

    tile = 32
    lane = lax.broadcasted_iota(jnp.int32, (tile, cols), 1)
    for number in range(PASSES):
        if number > 0:
            send_edges(number)
        backs[...] = jnp.zeros((up, cols), f32)

        def fold(k, carry):
            at_rows = pl.ds(pl.multiple_of(k * chunk, 128), chunk)
            flows = jnp.dot(fac[at_rows, :], ext[...], preferred_element_type=f32) - load[at_rows, :]
            lim = bound[at_rows, :]
            exc[...] = (flows - jnp.clip(flows, -lim, lim)).astype(bf16)
            backs[...] += jnp.dot(fact[:, at_rows], exc[...], preferred_element_type=f32)
            return carry

        lax.fori_loop(0, n_z, fold, 0)

        @pl.when(tm > 0)
        def _():
            edge_copy(number, 0).wait_recv()
            for g in range(4):
                e = erecv[number, 0]
                s = (-32 * g) % 128
                bef[g * (up // 4):(g + 1) * (up // 4), :] = pltpu.roll(e, s, 1) if s else e

        @pl.when(tm == 0)
        def _():
            bef[...] = pw[:, :128]

        @pl.when(tm < n_tm - 1)
        def _():
            edge_copy(number, 1).wait_recv()
            for g in range(4):
                e = erecv[number, 1]
                s = (96 - 32 * g) % 128
                aft[g * (up // 4):(g + 1) * (up // 4), :] = pltpu.roll(e, s, 1) if s else e

        @pl.when(tm == n_tm - 1)
        def _():
            aft[...] = pw[:, cols - 128:]

        balance = jnp.sum(pw[...], axis=0, keepdims=True) + total_row[...]
        balance_part = balance_weight * balance

        def update(i, carry):
            r = pl.ds(pl.multiple_of(i * tile, tile), tile)
            power = pw[r, :]
            commit = cm[r, :]
            linear = ut_ref[r, 0:1]
            quadratic = ut_ref[r, 1:2]
            capacity = ut_ref[r, 2:3]
            ramp_limit = ut_ref[r, 3:4]
            noload = ut_ref[r, 4:5]
            b = bef[r, :]
            a = aft[r, :]
            previous = jnp.where(lane < block, jnp.concatenate([b] * (cols // 128), axis=1), pltpu.roll(power, block, 1))
            nxt = jnp.where(lane >= cols - block, jnp.concatenate([a] * (cols // 128), axis=1), pltpu.roll(power, cols - block, 1))
            rate = power - previous
            over = rate - jnp.clip(rate, -ramp_limit, ramp_limit)
            coming = nxt - power
            following = coming - jnp.clip(coming, -ramp_limit, ramp_limit)
            ramp_term = over - following
            short = jnp.maximum(power - capacity * commit, 0.0)
            grad_power = (linear + 2.0 * quadratic * power + flow_weight * backs[r, :] + ramp_weight * ramp_term
                          + balance_part + short_weight * short)
            grad_commit = noload - short_weight * capacity * short + mult[r, :] + penalty * (commit - target[r, :])
            new_power = jnp.clip(power - step_power * grad_power, 0.0, capacity)
            pw[r, :] = new_power
            cm[r, :] = jnp.clip(commit - step_commit * grad_commit, 0.0, 1.0)
            ext[r, :] = new_power.astype(bf16)
            return carry

        lax.fori_loop(0, up // tile, update, 0)
        if number < PASSES - 1:
            store_edges(number + 1)

    psend[...] = lax.dot_general(hour_of, cm[...] + mult[...] / penalty, (((1,), (1,)), ((), ())),
                                 preferred_element_type=f32, precision=lax.Precision.HIGHEST)
    power_out[...] = pw[:units, :]
    commit_out[...] = cm[:units, :]

    def sum_copy(k):
        return pltpu.make_async_remote_copy(
            src_ref=psend, dst_ref=precv.at[scen], send_sem=psem_s.at[k], recv_sem=psem_r.at[scen],
            device_id=(tm, lax.rem(scen + k, n_scen)), device_id_type=MESH)

    for k in range(1, n_scen):
        sum_copy(k).start()
    precv[scen] = psend[...]
    for k in range(1, n_scen):
        src = lax.rem(scen + k, n_scen)
        pltpu.make_async_remote_copy(
            src_ref=psend, dst_ref=precv.at[src], send_sem=psem_s.at[k], recv_sem=psem_r.at[src],
            device_id=dev_x, device_id_type=MESH).wait_recv()
    totals = precv[0]
    for k in range(1, n_scen):
        totals = totals + precv[k]
    consensus = jnp.clip(totals / (block * n_scen), 0.0, 1.0)
    flipped = consensus.T
    cons_out[...] = flipped[:units, :]
    wide = jnp.dot(flipped, hour_of, preferred_element_type=f32, precision=lax.Precision.HIGHEST)
    upd_out[...] = (mult[...] + penalty * (cm[...] - wide))[:units, :]

    @pl.when(z > 0)
    def _():
        copy(own(mine), p_own, 0, dev_dn).wait_send()

    @pl.when(z < n_z - 1)
    def _():
        copy(own(mine), p_own, 1, dev_up).wait_send()

    copy(own(mine), p_own, 2, dev_x).wait_send()
    copy(own(other), p_own2, 2, dev_x).wait_send()

    def left(p, slot, dev):
        copy(at(p), p, slot, dev).wait_send()

    for k in range(1, n_z):
        for down in (True, False):
            zz = z - k if down else z + k

            @pl.when(zz >= 0 if down else zz < n_z)
            def _():
                p = piece(zz, x, mine)
                if down:
                    @pl.when(z < n_z - 1)
                    def _():
                        left(p, 1, dev_up)
                else:
                    @pl.when(z > 0)
                    def _():
                        left(p, 0, dev_dn)
                left(p, 2, dev_x)
                left(p, 3, dev_y)
                left(p, 4, dev_c)
                p = piece(zz, ox, mine)
                left(p, 3, dev_y)
                left(p, 4, dev_c)
                left(piece(zz, x, other), 4, dev_c)
                left(piece(zz, ox, other), 4, dev_c)
    for q in (mine, other):
        left(piece(z, ox, q), 4, dev_c)
    for k in range(1, n_scen):
        table_copy(k).wait_send()
        sum_copy(k).wait_send()
    for number in range(PASSES):
        @pl.when(tm < n_tm - 1)
        def _():
            edge_copy(number, 0).wait_send()

        @pl.when(tm > 0)
        def _():
            edge_copy(number, 1).wait_send()


def selection(unit_buses, wind_buses, buses, up, dtype):
    units = unit_buses.shape[0]
    wanted = jnp.concatenate([unit_buses, jnp.full((up - units,), -1, unit_buses.dtype), wind_buses])
    return (lax.broadcasted_iota(jnp.int32, (buses, wanted.shape[0]), 0) == wanted[None, :]).astype(dtype)


def fused(n_tm, n_scen, prior_dispatch, prior_commitment, prior_consensus, prior_multiplier, flow_factors,
          unit_buses, wind_buses, wind_output, demand, load_flows, line_limits, unit_table):
    units, cols = prior_dispatch.shape
    rows, buses = flow_factors.shape
    farms = wind_output.shape[0]
    up = -(-units // 128) * 128
    f32, bf16 = jnp.float32, jnp.bfloat16
    sel = jnp.dot(flow_factors, selection(unit_buses, wind_buses, buses, up, bf16), preferred_element_type=f32).astype(bf16)
    lanes = -(-rows // 128) * 128
    table = jnp.concatenate([load_flows.T, line_limits[None, :]], axis=0)
    table = jnp.pad(table, ((0, 16 - table.shape[0]), (0, lanes - rows)))
    cons = jnp.pad(prior_consensus, ((0, up - units), (0, 0)))
    ut = jnp.pad(unit_table.T, ((0, up - units), (0, 0)))
    need = jnp.repeat(demand, cols // H_DEV)[None, :]
    lines = rows * n_scen
    chunk = 2 * rows
    wide = up + farms
    vm = pl.BlockSpec(memory_space=pltpu.VMEM)
    dma = pltpu.SemaphoreType.DMA
    return pl.pallas_call(
        functools.partial(kernel, n_tm, n_scen, units),
        name="window",
        out_shape=(
            jax.ShapeDtypeStruct((units, cols), f32),
            jax.ShapeDtypeStruct((units, cols), f32),
            jax.ShapeDtypeStruct((units, H_DEV), f32),
            jax.ShapeDtypeStruct((units, cols), f32),
        ),
        in_specs=[vm] * 9,
        out_specs=(vm,) * 4,
        scratch_shapes=[
            pltpu.VMEM((lines, wide), bf16),
            pltpu.VMEM((up, lines), bf16),
            pltpu.VMEM((lines, cols), f32),
            pltpu.VMEM((lines, cols), f32),
            pltpu.VMEM((chunk, cols), bf16),
            pltpu.VMEM((up, cols), f32),
            pltpu.VMEM((up, cols), f32),
            pltpu.VMEM((up, cols), f32),
            pltpu.VMEM((up, cols), f32),
            pltpu.VMEM((wide, cols), bf16),
            pltpu.VMEM((up, cols), f32),
            pltpu.VMEM((up, 128), f32),
            pltpu.VMEM((up, 128), f32),
            pltpu.VMEM((n_scen, 16, lanes), bf16),
            pltpu.VMEM((PASSES, 2, up // 4, 128), f32),
            pltpu.VMEM((PASSES, 2, up // 4, 128), f32),
            pltpu.VMEM((H_DEV, up), f32),
            pltpu.VMEM((n_scen, H_DEV, up), f32),
            pltpu.VMEM((1, cols), f32),
            dma((n_scen * 4,)),
            dma((5, n_scen * 4)),
            dma((n_scen,)),
            dma((n_scen,)),
            dma((PASSES, 2)),
            dma((PASSES, 2)),
            dma((n_scen,)),
            dma((n_scen,)),
        ],
        compiler_params=pltpu.CompilerParams(collective_id=0, has_side_effects=True, vmem_limit_bytes=56 * 1024 * 1024),
    )(sel, table, prior_dispatch, prior_commitment, cons, prior_multiplier, wind_output, need, ut)


def passed_along(value, axis, steps):
    count = lax.axis_size(axis)
    first, last = (max(0, -steps), min(count, count - steps))
    return lax.ppermute(value, axis, [(source, source + steps) for source in range(first, last)])


def plain(prior_dispatch, prior_commitment, prior_consensus, prior_multiplier, flow_factors,
          unit_buses, wind_buses, wind_output, demand, load_flows, line_limits, unit_table):
    units, columns = prior_dispatch.shape
    block = columns // H_DEV
    linear, quadratic, capacity, ramp_limit, noload = (unit_table[i][:, None] for i in range(5))
    factors = jnp.dot(flow_factors, selection(unit_buses, wind_buses, flow_factors.shape[1], units, jnp.bfloat16),
                      preferred_element_type=jnp.float32).astype(jnp.bfloat16)
    wind_total = jnp.sum(wind_output.astype(jnp.float32), axis=0)
    needed = jnp.repeat(demand, block)
    target = jnp.repeat(prior_consensus, block, axis=1)
    first_block = lax.axis_index("tm") == 0
    last_block = lax.axis_index("tm") == lax.axis_size("tm") - 1
    power, commit = prior_dispatch, prior_commitment
    factors = lax.all_gather(factors, "scen", axis=0, tiled=True)
    hourly = jnp.repeat(lax.all_gather(load_flows, "scen", axis=0, tiled=True).astype(jnp.float32), block, axis=1)
    limit = lax.all_gather(line_limits, "scen", axis=0, tiled=True).astype(jnp.float32)[:, None]
    for _ in range(PASSES):
        extended = jnp.concatenate([power.astype(jnp.bfloat16), wind_output], axis=0)
        flows = jnp.dot(factors, extended, preferred_element_type=jnp.float32) - hourly
        excess = (flows - jnp.clip(flows, -limit, limit)).astype(jnp.bfloat16)
        back = lax.dot_general(factors[:, :units], excess, (((0,), (0,)), ((), ())), preferred_element_type=jnp.float32)
        before = passed_along(power[:, columns - block:], "tm", 1)
        after = passed_along(power[:, :block], "tm", -1)
        before = jnp.where(first_block, power[:, :block], before)
        after = jnp.where(last_block, power[:, columns - block:], after)
        rate = power - jnp.concatenate([before, power[:, :columns - block]], axis=1)
        coming = jnp.concatenate([power[:, block:], after], axis=1) - power
        over = rate - jnp.clip(rate, -ramp_limit, ramp_limit)
        following = coming - jnp.clip(coming, -ramp_limit, ramp_limit)
        balance = jnp.sum(power, axis=0) + wind_total - needed
        short = jnp.maximum(power - capacity * commit, 0.0)
        grad_power = (linear + 2.0 * quadratic * power + flow_weight * back + ramp_weight * (over - following)
                      + balance_weight * balance + short_weight * short)
        grad_commit = noload - short_weight * capacity * short + prior_multiplier + penalty * (commit - target)
        power, commit = (jnp.clip(power - step_power * grad_power, 0.0, capacity),
                         jnp.clip(commit - step_commit * grad_commit, 0.0, 1.0))
    sums = jnp.sum((commit + prior_multiplier / penalty).reshape(units, H_DEV, block), axis=2)
    totals = lax.psum(sums, "scen")
    consensus = jnp.clip(totals / (block * lax.axis_size("scen")), 0.0, 1.0)
    updated = prior_multiplier + penalty * (commit - jnp.repeat(consensus, block, axis=1))
    return power, commit, consensus, updated


def solution(mesh):
    n_tm, n_scen = mesh.shape["tm"], mesh.shape["scen"]

    def per_device(*args):
        rows, cols = args[4].shape[0], args[0].shape[1]
        fits = (n_tm == 4 and n_scen % 2 == 0 and rows % 64 == 0 and cols == 256
                and args[7].shape[0] % 128 == 0)
        if fits:
            return fused(n_tm, n_scen, *args)
        return plain(*args)

    both_axes = P(None, ("tm", "scen"))
    in_specs = (both_axes, both_axes, P(None, "tm"), both_axes, P("scen", None), P(), P(), both_axes,
                P("tm"), P("scen", "tm"), P("scen"), P())
    out_specs = (both_axes, both_axes, P(None, "tm"), both_axes)
    return jax.shard_map(per_device, mesh=mesh, in_specs=in_specs, out_specs=out_specs, check_vma=False)
```

time: 191 us -> 83.1 us (0.44)
  the two profiles are of different devices: /device:TPU:4 before, /device:TPU:1 now
where the time goes in v1:
time: 83.1 us; the launch traced here: 82.7 us
  Pallas kernels  66.9 us (81%)
  local copies, waits for them, and re-layouts  10.8 us (13%)
  matrix products  2.17 us (3%)
  other arithmetic  2.08 us (3%)
    pallas_call x1, Pallas kernels, fused(): pl.pallas_call(functools.partial(kernel, n_tm, n_scen, units), name='wind...  66.9 us
    unnamed x11, local copies, waits for them, and re-layouts  5.35 us
    dot_general x1, matrix products, fused(): jnp.dot(flow_factors, selection(unit_buses, wind_buses, buses, up, bf16),...  2.17 us
    pallas_call x1, local copies, waits for them, and re-layouts, fused(): pl.pallas_call(functools.partial(kernel, n_tm, n_scen, units), name='wind...  1.8 us

profile of v1, /device:TPU:1, one launch (start us, length us, event | category | flops | bytes accessed | tf_op | source)
XLA Modules:
  0.0 82.7 jit_solution(3463377982437775120)
XLA Ops:
  0.6 0.0 copy-start
  0.6 0.8 broadcast_in_dim.11
  1.4 0.8 pad_add_fusion
  2.2 0.7 broadcast_in_dim.12
  2.9 0.7 broadcast_in_dim_reshape.3.need_ref
  3.6 1.3 %fusion.9.tab_ref = bf16[16,384]{1,0:T(8,128)(2,1)} fusion(bf16[1,320]{1,0:T(2,128)(2,1)S(1)} %broadcast_in_dim.11, bf16[8,320]{1,0:T(8,128)(2,1)} %bitcast.6), kind=kLoop, calls=%fused_computation.12 | loop fusion | flops 67584 | bytes 18048 | tf_op jit(solution)/shard_map/concatenate | solution.py:426
  4.9 0.9 %copy.16 = f32[600,8]{1,0:T(8,128)S(1)} copy(f32[600,8]{0,1:T(8,128)} %param.14) | data formatting | bytes 38400 | tf_op args[2]
  5.8 0.8 pad.13.cons_ref
  6.5 0.9 %copy.17 = f32[5,600]{0,1:T(8,128)S(1)} copy(f32[5,600]{1,0:T(8,128)} %param.23) | data formatting | bytes 24000 | tf_op args[11]
  7.4 0.8 pad.14.ut_ref
  8.2 0.0 copy-done
  8.2 2.2 %fusion.3.sel_ref = bf16[320,768]{1,0:T(8,128)(2,1)} fusion(bf16[320,2000]{1,0:T(8,128)(2,1)S(1)} %copy-done, s32[768]{0:T(1024)S(1)} %pad_add_fusion), kind=kOutput, calls=%fused_computation.4 | convolution fusion | flops 984821760 | bytes 1774592 | tf_op jit(solution)/shard_map/dot_general | solution.py:424
  10.3 66.9 %window.1 = (f32[600,256]{1,0:T(8,128)}, f32[600,256]{1,0:T(8,128)}, f32[600,8]{1,0:T(8,128)}, f32[600,256]{1,0:T(8,128)}) custom-call(bf16[320,768]{1,0:T(8,128)(2,1)} %fusion.3.sel_ref, bf16[16,384]{1,0:T(8,128)(2,1)} %fusion.9.tab_ref, f32[600,256]{1,0:T(8,128)} %pd_ref.1, f32[600,256]{1,0:T(8,128)} %pc_ref.1, f32[640,8]{1,0:T(8,128)} %pad.13.cons_ref, ...), custom_call_target="tpu_custom_call" | custom-call | tf_op jit(solution)/shard_map/window/pallas_call | solution.py:436
  77.2 0.0 copy-start.2
  77.3 0.0 copy-start.1
  77.3 1.8 %copy.18 = f32[600,8]{0,1:T(8,128)} copy(f32[600,8]{1,0:T(8,128)} %get-tuple-element.6) | data formatting | bytes 38400 | tf_op jit(solution)/shard_map/window/pallas_call | solution.py:436
  79.1 1.9 %copy.22 = f32[600,256]{1,0:T(8,128)} copy(f32[600,256]{1,0:T(8,128)} %get-tuple-element.12) | data formatting | bytes 1228800
  81.0 0.0 copy-done.2
  81.0 0.8 copy.23
  81.8 0.0 copy-done.1
  81.8 0.8 copy.24
  (1 shorter events, 0.0 us)
Async XLA Ops:
  0.6 7.5 %copy-start = (bf16[320,2000]{1,0:T(8,128)(2,1)S(1)}, bf16[320,2000]{1,0:T(8,128)(2,1)}, u32[]{:S(2)}) copy-start(bf16[320,2000]{1,0:T(8,128)(2,1)} %param.16) | copy-start | bytes 3840004
  77.2 3.8 %copy-start.2 = (f32[600,256]{1,0:T(8,128)S(1)}, f32[600,256]{1,0:T(8,128)}, u32[]{:S(2)}) copy-start(f32[600,256]{1,0:T(8,128)} %get-tuple-element.13) | copy-start | bytes 1843204
  77.3 4.6 %copy-start.1 = (f32[600,256]{1,0:T(8,128)S(1)}, f32[600,256]{1,0:T(8,128)}, u32[]{:S(2)}) copy-start(f32[600,256]{1,0:T(8,128)} %get-tuple-element.15) | copy-start | bytes 1843204

commit v2 on v1

--- a/solution.py
+++ b/solution.py
@@ -20,10 +20,10 @@
 step_commit = 0.3
 
 
-def kernel(n_tm, n_scen, units, sel_ref, tab_ref, pd_ref, pc_ref, cons_ref, mu_ref, wind_ref, need_ref, ut_ref,
-           power_out, commit_out, cons_out, upd_out,
+def kernel(n_tm, n_scen, units, sel_ref, tab_ref, pd_ref, pc_ref, cons_ref, mu_ref, wind_ref, table_ref, need_ref,
+           power_out, commit_out, cons_out,
            fac, fact, load, bound, exc, pw, cm, mult, target, ext, backs, bef, aft,
-           tabs, esend, erecv, psend, precv, total_row,
+           tabs, esend, erecv, psend, precv, total_row, small, ut_ref,
            recv_sem, send_sem, tsend, trecv, esem_s, esem_r, psem_s, psem_r):
     rows = sel_ref.shape[0]
     quarter = rows // 4
@@ -145,13 +145,22 @@
     hour_row = lax.broadcasted_iota(jnp.int32, (H_DEV, cols), 0)
     hour_col = lax.broadcasted_iota(jnp.int32, (H_DEV, cols), 1)
     hour_of = ((hour_col >= hour_row * block) & (hour_col < hour_row * block + block)).astype(f32)
-    target[...] = jnp.dot(cons_ref[...], hour_of, preferred_element_type=f32, precision=lax.Precision.HIGHEST)
+    small[...] = jnp.zeros_like(small)
+    small[:, :units] = cons_ref[...]
+    target[...] = jnp.dot(small[...].T, hour_of, preferred_element_type=f32, precision=lax.Precision.HIGHEST)
+    small[...] = jnp.zeros_like(small)
+    small[:table_ref.shape[0], :units] = table_ref[...]
+    ut_ref[...] = small[...].T
     fac[pl.ds(pl.multiple_of(scen * rows, 16), rows), :] = sel_ref[...]
     tabs[scen] = tab_ref[...]
     ext[:up, :] = pw[...].astype(bf16)
     ext[up:, :] = wind_ref[...]
-    total_row[...] = jnp.sum(wind_ref[...].astype(f32), axis=0, keepdims=True) - need_ref[...]
+    needed = jnp.zeros((1, cols), f32)
+    for h in range(H_DEV):
+        needed = jnp.where(hour_of[h:h + 1] > 0.0, need_ref[h], needed)
+    total_row[...] = jnp.sum(wind_ref[...].astype(f32), axis=0, keepdims=True) - needed
     send_edges(0)
+    backs[...] = jnp.zeros((up, cols), f32)
 
     def along_z(k):
         for down in (True, False):
@@ -205,6 +214,45 @@
             arrived(p)
             pass_on(p, 4, dev_c)
 
+    def table_arrived(src):
+        pltpu.make_async_remote_copy(
+            src_ref=tab_ref, dst_ref=tabs.at[src], send_sem=tsend.at[0], recv_sem=trecv.at[src],
+            device_id=dev_x, device_id_type=MESH).wait_recv()
+
+    spread_row = lax.broadcasted_iota(jnp.int32, (H_DEV, cols), 0)
+    spread_col = lax.broadcasted_iota(jnp.int32, (H_DEV, cols), 1)
+    load_of = ((spread_col >= spread_row * block) & (spread_col < spread_row * block + block)).astype(bf16)
+    lines_first = (((0,), (0,)), ((), ()))
+
+    def line_step(at_rows):
+        flows = jnp.dot(fac[at_rows, :], ext[...], preferred_element_type=f32) - load[at_rows, :]
+        lim = bound[at_rows, :]
+        exc[at_rows, :] = (flows - jnp.clip(flows, -lim, lim)).astype(bf16)
+
+    def process(zz):
+        for xx in range(2):
+            s = zz * 2 + xx
+            at_rows = pl.ds(pl.multiple_of(s * rows, 16), rows)
+            load[at_rows, :] = lax.dot_general(tabs[s], load_of, lines_first, preferred_element_type=f32)
+            bound[at_rows, :] = jnp.broadcast_to(fac[at_rows, units:units + 1].astype(f32), (rows, cols))
+        at_rows = pl.ds(pl.multiple_of(zz * chunk, 128), chunk)
+        fact[:, at_rows] = fac[at_rows, :up].T
+        line_step(at_rows)
+        backs[...] += jnp.dot(fact[:, at_rows], exc[at_rows, :], preferred_element_type=f32)
+
+    def from_core(zz):
+        for xx in range(2):
+            for yy in range(2):
+                arrived(piece(zz, xx, yy * 2 + oc))
+            table_arrived(zz * 2 + xx)
+        process(zz)
+
+    def own_chunk():
+        for q in (oc, 2 + oc):
+            arrived(piece(z, ox, q))
+        table_arrived(z * 2 + ox)
+        process(z)
+
     along_z(1)
     own_plane_x()
     for k in range(2, n_z + 1):
@@ -214,61 +262,20 @@
         both(k - 1, from_y_same)
         if k > 2:
             both(k - 2, from_y_cross)
+            both(k - 2, from_core)
+        else:
+            own_chunk()
     both(n_z - 1, from_y_cross)
-
-    def from_core(zz):
-        for xx in range(2):
-            for yy in range(2):
-                arrived(piece(zz, xx, yy * 2 + oc))
-
-    for q in (oc, 2 + oc):
-        arrived(piece(z, ox, q))
-    for k in range(1, n_z):
-        both(k, from_core)
-    for k in range(1, n_scen):
-        src = lax.rem(scen + k, n_scen)
-        pltpu.make_async_remote_copy(
-            src_ref=tab_ref, dst_ref=tabs.at[src], send_sem=tsend.at[k], recv_sem=trecv.at[src],
-            device_id=dev_x, device_id_type=MESH).wait_recv()
-
-    spread_row = lax.broadcasted_iota(jnp.int32, (16, cols), 0)
-    spread_col = lax.broadcasted_iota(jnp.int32, (16, cols), 1)
-    load_of = ((spread_col >= spread_row * block) & (spread_col < spread_row * block + block)).astype(bf16)
-    limit_of = (spread_row == H_DEV).astype(bf16)
-    lines_first = (((0,), (0,)), ((), ()))
-
-    def prepare(s, carry):
-        table = tabs[s]
-        at_rows = pl.ds(pl.multiple_of(s * rows, 16), rows)
-        load[at_rows, :] = lax.dot_general(table, load_of, lines_first, preferred_element_type=f32)[:rows]
-        bound[at_rows, :] = lax.dot_general(table, limit_of, lines_first, preferred_element_type=f32)[:rows]
-        return carry
-
-    lax.fori_loop(0, n_scen, prepare, 0)
-
-    def flip(k, carry):
-        at_rows = pl.ds(pl.multiple_of(k * chunk, 128), chunk)
-        fact[:, at_rows] = fac[at_rows, :up].T
-        return carry
-
-    lax.fori_loop(0, n_z, flip, 0)
+    both(n_z - 1, from_core)
 
     tile = 32
     lane = lax.broadcasted_iota(jnp.int32, (tile, cols), 1)
     for number in range(PASSES):
         if number > 0:
             send_edges(number)
-        backs[...] = jnp.zeros((up, cols), f32)
-
-        def fold(k, carry):
-            at_rows = pl.ds(pl.multiple_of(k * chunk, 128), chunk)
-            flows = jnp.dot(fac[at_rows, :], ext[...], preferred_element_type=f32) - load[at_rows, :]
-            lim = bound[at_rows, :]
-            exc[...] = (flows - jnp.clip(flows, -lim, lim)).astype(bf16)
-            backs[...] += jnp.dot(fact[:, at_rows], exc[...], preferred_element_type=f32)
-            return carry
-
-        lax.fori_loop(0, n_z, fold, 0)
+            for k in range(n_z):
+                line_step(pl.ds(k * chunk, chunk))
+            backs[...] = jnp.dot(fact[...], exc[...], preferred_element_type=f32)
 
         @pl.when(tm > 0)
         def _():
@@ -351,10 +358,7 @@
     for k in range(1, n_scen):
         totals = totals + precv[k]
     consensus = jnp.clip(totals / (block * n_scen), 0.0, 1.0)
-    flipped = consensus.T
-    cons_out[...] = flipped[:units, :]
-    wide = jnp.dot(flipped, hour_of, preferred_element_type=f32, precision=lax.Precision.HIGHEST)
-    upd_out[...] = (mult[...] + penalty * (cm[...] - wide))[:units, :]
+    cons_out[...] = consensus
 
     @pl.when(z > 0)
     def _():
@@ -414,6 +418,20 @@
     return (lax.broadcasted_iota(jnp.int32, (buses, wanted.shape[0]), 0) == wanted[None, :]).astype(dtype)
 
 
+def finish(units, power_ref, commit_ref, mult_ref, cons_ref, power_out, commit_out, cons_out, upd_out):
+    cols = mult_ref.shape[1]
+    block = cols // H_DEV
+    hour_row = lax.broadcasted_iota(jnp.int32, (H_DEV, cols), 0)
+    hour_col = lax.broadcasted_iota(jnp.int32, (H_DEV, cols), 1)
+    hour_of = ((hour_col >= hour_row * block) & (hour_col < hour_row * block + block)).astype(jnp.float32)
+    wide = jnp.dot(cons_ref[...].T, hour_of, preferred_element_type=jnp.float32, precision=lax.Precision.HIGHEST)
+    power_out[...] = power_ref[...]
+    commit = commit_ref[...]
+    commit_out[...] = commit
+    cons_out[...] = cons_ref[:, :units]
+    upd_out[...] = mult_ref[...] + penalty * (commit - wide[:units, :])
+
+
 def fused(n_tm, n_scen, prior_dispatch, prior_commitment, prior_consensus, prior_multiplier, flow_factors,
           unit_buses, wind_buses, wind_output, demand, load_flows, line_limits, unit_table):
     units, cols = prior_dispatch.shape
@@ -422,34 +440,28 @@
     up = -(-units // 128) * 128
     f32, bf16 = jnp.float32, jnp.bfloat16
     sel = jnp.dot(flow_factors, selection(unit_buses, wind_buses, buses, up, bf16), preferred_element_type=f32).astype(bf16)
-    lanes = -(-rows // 128) * 128
-    table = jnp.concatenate([load_flows.T, line_limits[None, :]], axis=0)
-    table = jnp.pad(table, ((0, 16 - table.shape[0]), (0, lanes - rows)))
-    cons = jnp.pad(prior_consensus, ((0, up - units), (0, 0)))
-    ut = jnp.pad(unit_table.T, ((0, up - units), (0, 0)))
-    need = jnp.repeat(demand, cols // H_DEV)[None, :]
+    column = lax.broadcasted_iota(jnp.int32, sel.shape, 1)
+    sel = jnp.where(column == units, line_limits[:, None], sel)
     lines = rows * n_scen
-    chunk = 2 * rows
     wide = up + farms
     vm = pl.BlockSpec(memory_space=pltpu.VMEM)
     dma = pltpu.SemaphoreType.DMA
-    return pl.pallas_call(
+    power, commit, cons = pl.pallas_call(
         functools.partial(kernel, n_tm, n_scen, units),
         name="window",
         out_shape=(
             jax.ShapeDtypeStruct((units, cols), f32),
             jax.ShapeDtypeStruct((units, cols), f32),
-            jax.ShapeDtypeStruct((units, H_DEV), f32),
-            jax.ShapeDtypeStruct((units, cols), f32),
+            jax.ShapeDtypeStruct((H_DEV, up), f32),
         ),
-        in_specs=[vm] * 9,
-        out_specs=(vm,) * 4,
+        in_specs=[vm] * 8 + [pl.BlockSpec(memory_space=pltpu.SMEM)],
+        out_specs=(vm,) * 3,
         scratch_shapes=[
             pltpu.VMEM((lines, wide), bf16),
             pltpu.VMEM((up, lines), bf16),
             pltpu.VMEM((lines, cols), f32),
             pltpu.VMEM((lines, cols), f32),
-            pltpu.VMEM((chunk, cols), bf16),
+            pltpu.VMEM((lines, cols), bf16),
             pltpu.VMEM((up, cols), f32),
             pltpu.VMEM((up, cols), f32),
             pltpu.VMEM((up, cols), f32),
@@ -458,12 +470,14 @@
             pltpu.VMEM((up, cols), f32),
             pltpu.VMEM((up, 128), f32),
             pltpu.VMEM((up, 128), f32),
-            pltpu.VMEM((n_scen, 16, lanes), bf16),
+            pltpu.VMEM((n_scen, H_DEV, rows), bf16),
             pltpu.VMEM((PASSES, 2, up // 4, 128), f32),
             pltpu.VMEM((PASSES, 2, up // 4, 128), f32),
             pltpu.VMEM((H_DEV, up), f32),
             pltpu.VMEM((n_scen, H_DEV, up), f32),
             pltpu.VMEM((1, cols), f32),
+            pltpu.VMEM((H_DEV, up), f32),
+            pltpu.VMEM((up, H_DEV), f32),
             dma((n_scen * 4,)),
             dma((5, n_scen * 4)),
             dma((n_scen,)),
@@ -474,7 +488,20 @@
             dma((n_scen,)),
         ],
         compiler_params=pltpu.CompilerParams(collective_id=0, has_side_effects=True, vmem_limit_bytes=56 * 1024 * 1024),
-    )(sel, table, prior_dispatch, prior_commitment, cons, prior_multiplier, wind_output, need, ut)
+    )(sel, load_flows.T, prior_dispatch, prior_commitment, prior_consensus.T, prior_multiplier, wind_output, unit_table, demand)
+    power, commit, cons, updated = pl.pallas_call(
+        functools.partial(finish, units),
+        name="finish",
+        out_shape=(
+            jax.ShapeDtypeStruct((units, cols), f32),
+            jax.ShapeDtypeStruct((units, cols), f32),
+            jax.ShapeDtypeStruct((H_DEV, units), f32),
+            jax.ShapeDtypeStruct((units, cols), f32),
+        ),
+        in_specs=[vm] * 4,
+        out_specs=(vm,) * 4,
+    )(power, commit, prior_multiplier, cons)
+    return power, commit, cons.T, updated
 
 
 def passed_along(value, axis, steps):
@@ -532,7 +559,7 @@
     def per_device(*args):
         rows, cols = args[4].shape[0], args[0].shape[1]
         fits = (n_tm == 4 and n_scen % 2 == 0 and rows % 64 == 0 and cols == 256
-                and args[7].shape[0] % 128 == 0)
+                and args[7].shape[0] % 128 == 0 and args[0].shape[0] % 128 > 0)
         if fits:
             return fused(n_tm, n_scen, *args)
         return plain(*args)

time: 83.1 us -> 64.5 us (0.78)
  local copies, waits for them, and re-layouts: 10.8 us -> 0.45 us
  Pallas kernels: 66.9 us -> 59.5 us
  other arithmetic: 2.08 us -> 0.89 us
    pallas_call x1, Pallas kernels: 66.9 us -> 56.2 us  [fused(): pl.pallas_call(functools.partial(kernel, n_tm, n_scen, units), name='wind...]
    unnamed x11 -> x2, local copies, waits for them, and re-layouts: 5.35 us -> 0.44 us
    pallas_call x0 -> x1, Pallas kernels: none -> 3.33 us  [fused(): pl.pallas_call(functools.partial(finish, units), name='finish', out_shape...]
    pallas_call x1 -> x0, local copies, waits for them, and re-layouts: 1.8 us -> none  [fused(): pl.pallas_call(functools.partial(kernel, n_tm, n_scen, units), name='wind...]
    broadcast_in_dim x2 -> x0, local copies, waits for them, and re-layouts: 1.51 us -> none  [the longest x1 0.79 us: fused(): table = jnp.concatenate([load_flows.T, line_limits[None, :]], axis=0)]
    pad x2 -> x0, local copies, waits for them, and re-layouts: 1.51 us -> none  [the longest x1 0.75 us: fused(): cons = jnp.pad(prior_consensus, ((0, up - units), (0, 0)))]
    concatenate x1 -> x0, other arithmetic: 1.3 us -> none  [fused(): table = jnp.concatenate([load_flows.T, line_limits[None, :]], axis=0)]
where the time goes in v2:
time: 64.5 us; the launch traced here: 64.3 us
  Pallas kernels  59.5 us (92%)
  matrix products  2.85 us (4%)
  other arithmetic  0.89 us (1%)
  between operations  0.66 us (1%)
    pallas_call x1, Pallas kernels, fused(): pl.pallas_call(functools.partial(kernel, n_tm, n_scen, units), name='wind...  56.2 us
    pallas_call x1, Pallas kernels, fused(): pl.pallas_call(functools.partial(finish, units), name='finish', out_shape...  3.33 us
    dot_general x1, matrix products, fused(): jnp.dot(flow_factors, selection(unit_buses, wind_buses, buses, up, bf16),...  2.85 us

profile of v2, /device:TPU:1, one launch (start us, length us, event | category | flops | bytes accessed | tf_op | source)
XLA Modules:
  0.0 64.3 jit_solution(4646125391952924195)
XLA Ops:
  0.6 0.0 copy-start
  0.7 0.9 %pad_add_fusion = s32[768]{0:T(1024)S(1)} fusion(s32[128]{0:T(128)} %param.18, s32[40]{0:T(128)S(1)} %broadcast_in_dim.14, s32[600]{0:T(1024)} %param.17), kind=kLoop, calls=%fused_computation.6 | loop fusion | flops 1536 | bytes 6144 | tf_op jit(solution)/shard_map/concatenate | solution.py:417
  1.5 0.4 copy-done
  2.0 2.9 %fusion.4.sel_ref = bf16[320,768]{1,0:T(8,128)(2,1)} fusion(bf16[320,2000]{1,0:T(8,128)(2,1)S(1)} %copy-done, s32[768]{0:T(1024)S(1)} %pad_add_fusion, pred[768]{0:T(1024)(128)(4,1)S(1)} %iota_compare_fusion.8, bf16[320]{0:T(512)(128)(2,1)} %param.22), kind=kOutput, calls=%fused_computation.5 | convolution fusion | flops 985067520 | bytes 1776000 | tf_op jit(solution)/shard_map/dot_general | solution.py:442
  4.8 56.2 %window.1 = (f32[600,256]{1,0:T(8,128)}, f32[600,256]{1,0:T(8,128)}, f32[8,640]{1,0:T(8,128)}) custom-call(bf16[320,768]{1,0:T(8,128)(2,1)} %fusion.4.sel_ref, bf16[8,320]{1,0:T(8,128)(2,1)} %bitcast.7, f32[600,256]{1,0:T(8,128)} %pd_ref.1, f32[600,256]{1,0:T(8,128)} %pc_ref.1, f32[8,600]{1,0:T(8,128)} %bitcast.6, f32[600,256]{1,0:T(8,128)} %mult_ref.1, ...), custom_call_target="tpu_custom_call" | custom-call | tf_op jit(solution)/shard_map/window/pallas_call | solution.py:449
  61.0 3.3 %finish.1 = (f32[600,256]{1,0:T(8,128)}, f32[600,256]{1,0:T(8,128)}, f32[8,600]{1,0:T(8,128)}, f32[600,256]{1,0:T(8,128)}) custom-call(f32[600,256]{1,0:T(8,128)} %get-tuple-element.11.power_ref, f32[600,256]{1,0:T(8,128)} %get-tuple-element.12.commit_ref, f32[600,256]{1,0:T(8,128)} %mult_ref.1, f32[8,640]{1,0:T(8,128)} %get-tuple-element.13.cons_ref), custom_call_target="tpu_custom_call" | custom-call | tf_op jit(solution)/shard_map/finish/pallas_call | solution.py:492
  (2 shorter events, 0.0 us)
Async XLA Ops:
  0.6 1.4 %copy-start = (bf16[320,2000]{1,0:T(8,128)(2,1)S(1)}, bf16[320,2000]{1,0:T(8,128)(2,1)}, u32[]{:S(2)}) copy-start(bf16[320,2000]{1,0:T(8,128)(2,1)} %param.16) | copy-start | bytes 3840004

commit v3 on v2

--- a/solution.py
+++ b/solution.py
@@ -18,6 +18,13 @@
 penalty = 1.0
 step_power = 0.2
 step_commit = 0.3
+
+
+def split(value):
+    high = value.astype(jnp.bfloat16)
+    rest = value - high.astype(jnp.float32)
+    middle = rest.astype(jnp.bfloat16)
+    return high, middle, (rest - middle.astype(jnp.float32)).astype(jnp.bfloat16)
 
 
 def kernel(n_tm, n_scen, units, sel_ref, tab_ref, pd_ref, pc_ref, cons_ref, mu_ref, wind_ref, table_ref, need_ref,
@@ -332,14 +339,15 @@
             ext[r, :] = new_power.astype(bf16)
             return carry
 
-        lax.fori_loop(0, up // tile, update, 0)
+        lax.fori_loop(0, up // tile, update, 0, unroll=4)
         if number < PASSES - 1:
             store_edges(number + 1)
 
-    psend[...] = lax.dot_general(hour_of, cm[...] + mult[...] / penalty, (((1,), (1,)), ((), ())),
-                                 preferred_element_type=f32, precision=lax.Precision.HIGHEST)
-    power_out[...] = pw[:units, :]
-    commit_out[...] = cm[:units, :]
+    spread = hour_of.astype(bf16)
+    sums = jnp.zeros((H_DEV, up), f32)
+    for part in split(cm[...] + mult[...] / penalty):
+        sums = sums + lax.dot_general(spread, part, (((1,), (1,)), ((), ())), preferred_element_type=f32)
+    psend[...] = sums
 
     def sum_copy(k):
         return pltpu.make_async_remote_copy(
@@ -349,6 +357,8 @@
     for k in range(1, n_scen):
         sum_copy(k).start()
     precv[scen] = psend[...]
+    power_out[...] = pw[:units, :]
+    commit_out[...] = cm[:units, :]
     for k in range(1, n_scen):
         src = lax.rem(scen + k, n_scen)
         pltpu.make_async_remote_copy(
@@ -418,18 +428,27 @@
     return (lax.broadcasted_iota(jnp.int32, (buses, wanted.shape[0]), 0) == wanted[None, :]).astype(dtype)
 
 
-def finish(units, power_ref, commit_ref, mult_ref, cons_ref, power_out, commit_out, cons_out, upd_out):
-    cols = mult_ref.shape[1]
+def finish(units, power_ref, commit_ref, mult_ref, cons_ref, power_out, commit_out, cons_out, upd_out, parts):
+    tile, cols = mult_ref.shape
     block = cols // H_DEV
+    step = pl.program_id(0)
+
+    @pl.when(step == 0)
+    def _():
+        cons = cons_ref[...]
+        cons_out[...] = cons[:, :units]
+        parts[...] = jnp.concatenate([part.astype(jnp.float32) for part in split(cons)], axis=0).T
+
     hour_row = lax.broadcasted_iota(jnp.int32, (H_DEV, cols), 0)
     hour_col = lax.broadcasted_iota(jnp.int32, (H_DEV, cols), 1)
     hour_of = ((hour_col >= hour_row * block) & (hour_col < hour_row * block + block)).astype(jnp.float32)
-    wide = jnp.dot(cons_ref[...].T, hour_of, preferred_element_type=jnp.float32, precision=lax.Precision.HIGHEST)
+    spread = jnp.concatenate([hour_of] * 3, axis=0).astype(jnp.bfloat16)
+    mine = parts[pl.ds(pl.multiple_of(step * tile, 8), tile), :].astype(jnp.bfloat16)
+    wide = jnp.dot(mine, spread, preferred_element_type=jnp.float32)
     power_out[...] = power_ref[...]
     commit = commit_ref[...]
     commit_out[...] = commit
-    cons_out[...] = cons_ref[:, :units]
-    upd_out[...] = mult_ref[...] + penalty * (commit - wide[:units, :])
+    upd_out[...] = mult_ref[...] + penalty * (commit - wide)
 
 
 def fused(n_tm, n_scen, prior_dispatch, prior_commitment, prior_consensus, prior_multiplier, flow_factors,
@@ -489,6 +508,8 @@
         ],
         compiler_params=pltpu.CompilerParams(collective_id=0, has_side_effects=True, vmem_limit_bytes=56 * 1024 * 1024),
     )(sel, load_flows.T, prior_dispatch, prior_commitment, prior_consensus.T, prior_multiplier, wind_output, unit_table, demand)
+    steps = 1
+    tiles = pl.BlockSpec((units // steps, cols), lambda i: (i, 0))
     power, commit, cons, updated = pl.pallas_call(
         functools.partial(finish, units),
         name="finish",
@@ -498,8 +519,10 @@
             jax.ShapeDtypeStruct((H_DEV, units), f32),
             jax.ShapeDtypeStruct((units, cols), f32),
         ),
-        in_specs=[vm] * 4,
-        out_specs=(vm,) * 4,
+        grid=(steps,),
+        in_specs=[tiles, tiles, tiles, pl.BlockSpec((H_DEV, up), lambda i: (0, 0))],
+        out_specs=(tiles, tiles, pl.BlockSpec((H_DEV, units), lambda i: (0, 0)), tiles),
+        scratch_shapes=[pltpu.VMEM((up, 3 * H_DEV), f32)],
     )(power, commit, prior_multiplier, cons)
     return power, commit, cons.T, updated
 

time: 64.5 us -> 62.4 us (0.967)
  Pallas kernels: 59.5 us -> 57.3 us
    pallas_call x1, Pallas kernels: 56.2 us -> 54.4 us  [fused(): pl.pallas_call(functools.partial(kernel, n_tm, n_scen, units), name='wind...]
where the time goes in v3:
time: 62.4 us; the launch traced here: 62.1 us
  Pallas kernels  57.3 us (92%)
  matrix products  2.85 us (5%)
  other arithmetic  0.89 us (1%)
  between operations  0.66 us (1%)
    pallas_call x1, Pallas kernels, fused(): pl.pallas_call(functools.partial(kernel, n_tm, n_scen, units), name='wind...  54.4 us
    pallas_call x1, Pallas kernels, fused(): pl.pallas_call(functools.partial(finish, units), name='finish', out_shape...  2.91 us
    dot_general x1, matrix products, fused(): jnp.dot(flow_factors, selection(unit_buses, wind_buses, buses, up, bf16),...  2.85 us

profile of v3, /device:TPU:1, one launch (start us, length us, event | category | flops | bytes accessed | tf_op | source)
XLA Modules:
  0.0 62.1 jit_solution(2536757919389300870)
XLA Ops:
  0.6 0.0 copy-start
  0.7 0.9 %pad_add_fusion = s32[768]{0:T(1024)S(1)} fusion(s32[128]{0:T(128)} %param.18, s32[40]{0:T(128)S(1)} %broadcast_in_dim.14, s32[600]{0:T(1024)} %param.17), kind=kLoop, calls=%fused_computation.6 | loop fusion | flops 1536 | bytes 6144 | tf_op jit(solution)/shard_map/concatenate | solution.py:427
  1.5 0.4 copy-done
  2.0 2.9 %fusion.4.sel_ref = bf16[320,768]{1,0:T(8,128)(2,1)} fusion(bf16[320,2000]{1,0:T(8,128)(2,1)S(1)} %copy-done, s32[768]{0:T(1024)S(1)} %pad_add_fusion, pred[768]{0:T(1024)(128)(4,1)S(1)} %iota_compare_fusion.8, bf16[320]{0:T(512)(128)(2,1)} %param.22), kind=kOutput, calls=%fused_computation.5 | convolution fusion | flops 985067520 | bytes 1776000 | tf_op jit(solution)/shard_map/dot_general | solution.py:461
  4.8 54.4 %window.1 = (f32[600,256]{1,0:T(8,128)}, f32[600,256]{1,0:T(8,128)}, f32[8,640]{1,0:T(8,128)}) custom-call(bf16[320,768]{1,0:T(8,128)(2,1)} %fusion.4.sel_ref, bf16[8,320]{1,0:T(8,128)(2,1)} %bitcast.7, f32[600,256]{1,0:T(8,128)} %pd_ref.1, f32[600,256]{1,0:T(8,128)} %pc_ref.1, f32[8,600]{1,0:T(8,128)} %bitcast.6, f32[600,256]{1,0:T(8,128)} %mult_ref.1, ...), custom_call_target="tpu_custom_call" | custom-call | tf_op jit(solution)/shard_map/window/pallas_call | solution.py:468
  59.2 2.9 %finish.1 = (f32[600,256]{1,0:T(8,128)}, f32[600,256]{1,0:T(8,128)}, f32[8,600]{1,0:T(8,128)}, f32[600,256]{1,0:T(8,128)}) custom-call(f32[600,256]{1,0:T(8,128)} %get-tuple-element.11.power_ref, f32[600,256]{1,0:T(8,128)} %get-tuple-element.12.commit_ref, f32[600,256]{1,0:T(8,128)} %mult_ref.1, f32[8,640]{1,0:T(8,128)} %get-tuple-element.13.cons_ref), custom_call_target="tpu_custom_call" | custom-call | tf_op jit(solution)/shard_map/finish/pallas_call | solution.py:513
  (2 shorter events, 0.0 us)
Async XLA Ops:
  0.6 1.4 %copy-start = (bf16[320,2000]{1,0:T(8,128)(2,1)S(1)}, bf16[320,2000]{1,0:T(8,128)(2,1)}, u32[]{:S(2)}) copy-start(bf16[320,2000]{1,0:T(8,128)(2,1)} %param.16) | copy-start | bytes 3840004
